TPU v7x, 32 devices: a whole 2x2x4 slice. The times are simulated.
32 devices in a mesh: seq: 4 (over z), phase: 4 (over y, x), dp: 2 (over core).
Axes of the slice: x: 2, y: 2, z: 4, core: 2. Of those that a mesh axis runs over, the one named last changes fastest.
Arguments:
- byte_embed: bfloat16 [4096, 1536], P(('dp', 'seq')), parts along dimension 0, may hold values from -6 to 6
- in_gain: float32 [1536], replicated, may hold values from 0.25 to 1.75
- w_qkv: bfloat16 [1536, 3, 1536], P('seq', None, 'phase')
- w_up: bfloat16 [1536, 3072], P('phase')
- out_gain: float32 [3072], P('phase'), may hold values from 0.25 to 1.75
- bounds: int32 [1024], P(('dp', 'seq')), parts along dimension 0, may hold values from 0 to 2047, as said below
- owner: int32 [1024, 1], P(('dp', 'seq')), parts along dimension 0, may hold values from 0 to 3; in each aligned block of 128 rows (0 to 127, 128 to 255, ...) at most 64 rows name the same one
Outputs:
- byte_states: bfloat16 [4096, 1536], P(('dp', 'seq'), 'phase'), parts along dimension 0
- stretch_states: bfloat16 [2048, 3072], P(('dp', 'seq'), 'phase'), parts along dimension 0
There are 2 independent parts, one for each index of `dp`. A program takes and returns all parts, laid end to end along the dimension named above; an argument that names none is the same for every part. Nothing has to cross between parts.
Inputs may be any that keep to these rules, and one draw needn't show every extreme that they name: `bounds`: strictly rising; the 128 entries of block b lie in bytes b * 512 to (b + 1) * 512 - 1, and the first and last byte of each block are among them. Among the 128 stretch rows of one block no owner is named more than 64 times.
All inputs are finite; a program needn't handle non-finite values.
Results may differ from a plain program's by a relative error of at most 0.013.
Values may be sent and summed in bfloat16 or wider, within the bound.
A program may use at most 128 MiB of HBM per device.

v0:
```python
import jax
import jax.numpy as jnp
from jax import lax
from jax.sharding import PartitionSpec as P

DC = 3072
HD = 128
WINDOW = 1024


def passed_along(value, axis, by):
    devices = lax.axis_size(axis)
    pairs = [(i, i + by) for i in range(devices) if 0 <= i + by < devices]
    return lax.ppermute(value, axis, pairs)


def project_rows(rows, w_up, out_gain):
    groups = lax.axis_size("phase")
    full_rows = lax.all_gather(rows, "phase", axis=1, tiled=True)
    w_cols = lax.all_to_all(w_up, "phase", split_axis=1, concat_axis=0, tiled=True)
    count = full_rows.shape[0]
    width = rows.shape[1]
    columns = w_cols.shape[1]
    pieces = jnp.einsum(
        "nsg,sgc->snc",
        full_rows.reshape(count, groups, width),
        w_cols.reshape(groups, width, columns),
        preferred_element_type=jnp.float32,
    )
    projected = jnp.sum(pieces.astype(jnp.bfloat16).astype(jnp.float32), axis=0)
    squares = lax.psum(jnp.sum(projected * projected, axis=1), "phase")
    scale = lax.rsqrt(squares / DC + 1e-05)
    return (projected * scale[:, None] * out_gain).astype(jnp.bfloat16)


def on_device(byte_embed, in_gain, w_qkv, w_up, out_gain, bounds, owner):
    tok = byte_embed.shape[0]
    n_seq = lax.axis_size("seq")
    mine = lax.axis_index("seq")
    section = lax.axis_index("phase")
    width_dev = w_qkv.shape[2]
    heads_dev = width_dev // HD
    x32 = byte_embed.astype(jnp.float32)
    normed = (x32 * lax.rsqrt(jnp.mean(x32 * x32, axis=1, keepdims=True) + 1e-05) * in_gain).astype(
        jnp.bfloat16
    )
    piece = lax.all_gather(w_qkv, "seq", axis=0, tiled=True)
    qkv = jnp.dot(
        normed, piece.reshape(piece.shape[0], 3 * width_dev), preferred_element_type=jnp.float32
    ).astype(jnp.bfloat16)
    qkv = qkv.reshape(tok, 3, heads_dev, HD)
    query = qkv[:, 0]
    keys = qkv[:, 1]
    values = qkv[:, 2]
    reach = -(-WINDOW // tok)
    key_list = [keys]
    value_list = [values]
    for distance in range(1, reach + 1):
        earlier_keys, earlier_values = passed_along((keys, values), "seq", distance)
        key_list = [earlier_keys] + key_list
        value_list = [earlier_values] + value_list
    key_all = jnp.concatenate(key_list, axis=0)
    value_all = jnp.concatenate(value_list, axis=0)
    scores = jnp.einsum(
        "ihd,jhd->hij", query, key_all, preferred_element_type=jnp.float32
    ) * HD ** (-0.5)
    q_pos = mine * tok + jnp.arange(tok, dtype=jnp.int32)
    k_pos = mine * tok - reach * tok + jnp.arange((reach + 1) * tok, dtype=jnp.int32)
    keep = (
        (k_pos[None, :] <= q_pos[:, None])
        & (k_pos[None, :] > q_pos[:, None] - WINDOW)
        & (k_pos[None, :] >= 0)
    )
    scores = jnp.where(keep[None], scores, -jnp.inf)
    top = jnp.max(scores, axis=2, keepdims=True)
    expo = jnp.exp(scores - top)
    probs = (expo / jnp.sum(expo, axis=2, keepdims=True)).astype(jnp.bfloat16)
    attended = jnp.einsum(
        "hij,jhd->ihd", probs, value_all, preferred_element_type=jnp.float32
    ).astype(jnp.bfloat16)
    attended = attended.reshape(tok, width_dev)
    residual = lax.dynamic_slice_in_dim(x32, section * width_dev, width_dev, 1)
    byte_states = (residual + attended.astype(jnp.float32)).astype(jnp.bfloat16)
    local = bounds - mine * tok
    stretch_rows = jnp.take(byte_states, local, axis=0)
    owners = owner[:, 0]
    crows = owners.shape[0]
    slot_count = 2 * crows // n_seq
    place = jnp.arange(crows, dtype=jnp.int32)
    earlier = (owners[:, None] == owners[None, :]) & (place[None, :] < place[:, None])
    rank = jnp.sum(earlier.astype(jnp.int32), axis=1)
    target = owners * slot_count + rank
    placing = (target[None, :] == jnp.arange(n_seq * slot_count, dtype=jnp.int32)[:, None]).astype(
        jnp.bfloat16
    )
    outgoing = jnp.dot(placing, stretch_rows, preferred_element_type=jnp.float32).astype(
        jnp.bfloat16
    )
    outgoing = outgoing.reshape(n_seq, slot_count, width_dev)
    arrived = lax.all_to_all(outgoing, "seq", split_axis=0, concat_axis=0, tiled=True).reshape(
        n_seq * slot_count, width_dev
    )
    stretch_states = project_rows(arrived, w_up, out_gain)
    return (byte_states, stretch_states)


def solution(mesh):
    return jax.shard_map(
        on_device,
        mesh=mesh,
        in_specs=(
            P(("dp", "seq"), None),
            P(),
            P("seq", None, "phase"),
            P("phase", None),
            P("phase"),
            P(("dp", "seq")),
            P(("dp", "seq"), None),
        ),
        out_specs=(P(("dp", "seq"), "phase"), P(("dp", "seq"), "phase")),
        check_vma=False,
    )
```

profile of v0, /device:TPU:0, one launch (start us, length us, event | category | flops | bytes accessed | tf_op | source)
XLA Modules:
  0.0 220.7 jit_solution(122934458647829781)
XLA Ops:
  7.2 2.4 %copy.31 = bf16[384,3,384]{0,2,1:T(8,128)(2,1)} copy(bf16[384,3,384]{2,0,1:T(8,128)(2,1)} %param.9) | data formatting | bytes 1769472 | tf_op args[2]
  9.7 2.0 convert_element_type.44
  12.4 69.8 %all-gather.2.cloned.1.call-done = bf16[1536,3,384]{0,2,1:T(8,128)(2,1)} async-done(((bf16[384,3,384]{0,2,1:T(8,128)(2,1)}), bf16[1536,3,384]{0,2,1:T(8,128)(2,1)}) %all-gather.2.cloned.1.call-update) | async-done | bytes 3538960 | tf_op jit(solution)/shard_map/all_gather | solution.py:47
  82.2 4.3 %convolution_convert_fusion = bf16[512,1152]{1,0:T(8,128)(2,1)S(1)} fusion(bf16[1536,1152]{0,1:T(8,128)(2,1)} %bitcast.36, f32[1536]{0:T(1024)S(1)} %copy-done.5, f32[512]{0:T(512)S(1)} %add_rsqrt_fusion, bf16[512,1536]{1,0:T(8,128)(2,1)S(1)} %copy-done), kind=kOutput, calls=%fused_computation.14 | convolution fusion | flops 1815674880 | bytes 6299648 | tf_op jit(solution)/shard_map/dot_general | solution.py:48
  88.2 2.9 %collective-permute-start.2 = (bf16[512,3,128]{2,0,1:T(8,128)(2,1)S(1)}, bf16[512,3,128]{2,0,1:T(8,128)(2,1)S(1)}, u32[]{:S(2)}, u32[]{:S(2)}) collective-permute-start(bf16[512,3,128]{2,0,1:T(8,128)(2,1)S(1)} %bitcast.30), channel_id=1, source_target_pairs={{0,16},{8,24},{1,17},{9,25},{2,18},{10,26},{3,19},{11,27},{4,20},{... | collective-permute-start | bytes 1179656 | tf_op jit(solution)/shard_map/ppermute | solution.py:14
  91.1 2.4 %collective-permute-start.3 = (bf16[512,3,128]{2,0,1:T(8,128)(2,1)S(1)}, bf16[512,3,128]{2,0,1:T(8,128)(2,1)S(1)}, u32[]{:S(2)}, u32[]{:S(2)}) collective-permute-start(bf16[512,3,128]{2,0,1:T(8,128)(2,1)S(1)} %bitcast.31), channel_id=1, source_target_pairs={{0,8},{8,16},{16,24},{1,9},{9,17},{17,25},{2,10},{10,18},{18,26},{... | collective-permute-start | bytes 1179656 | tf_op jit(solution)/shard_map/ppermute | solution.py:14
  93.6 1.7 and_and_fusion
  95.3 2.0 collective-permute-start
  97.3 2.7 %collective-permute-start.1 = (bf16[512,3,128]{0,2,1:T(8,128)(2,1)}, bf16[512,3,128]{0,2,1:T(8,128)(2,1)}, u32[]{:S(2)}, u32[]{:S(2)}) collective-permute-start(bf16[512,3,128]{0,2,1:T(8,128)(2,1)} %get-tuple-element.4), channel_id=1, source_target_pairs={{0,8},{8,16},{16,24},{1,9},{9,17},{17,25},{2,10},{10,18},{18,26},{... | collective-permute-start | bytes 1179656 | tf_op jit(solution)/shard_map/ppermute | solution.py:14
  100.6 8.4 %collective-permute-done.3 = bf16[512,3,128]{2,0,1:T(8,128)(2,1)S(1)} collective-permute-done((bf16[512,3,128]{2,0,1:T(8,128)(2,1)S(1)}, bf16[512,3,128]{2,0,1:T(8,128)(2,1)S(1)}, u32[]{:S(2)}, u32[]{:S(2)}) %collective-permute-start.3) | collective-permute-done | bytes 393248 | tf_op jit(solution)/shard_map/ppermute | solution.py:14
  109.0 2.4 %fusion.21 = f32[3,512,1536]{2,1,0:T(8,128)S(1)} fusion(bf16[512,3,128]{2,0,1:T(8,128)(2,1)S(1)} %bitcast.32, bf16[512,3,128]{2,0,1:T(8,128)(2,1)S(1)} %collective-permute-done.3, bf16[512,3,128]{2,0,1:T(8,128)(2,1)S(1)} %collective-permute-done.2, bf16[512,3,3,128]{0,3,2,1:T(8,128)(2,1)} %bitcast.29), kind=kOutput, calls=%fused_computation.28 | convolution fusion | flops 607518720 | bytes 11010048 | tf_op jit(solution)/shard_map/ihd,jhd->hij/dot_general | solution.py:64
  111.4 9.4 %fusion.39 = (f32[3,512]{1,0:T(4,128)S(1)}, f32[3,512,1536]{2,1,0:T(8,128)}) fusion(f32[3,512,1536]{2,1,0:T(8,128)S(1)} %fusion.21, pred[512,1536]{1,0:T(8,128)(4,1)} %and_and_fusion), kind=kOutput, calls=%fused_computation.63 | output fusion | flops 14157311 | bytes 19666944 | tf_op jit(solution)/shard_map/sub | solution.py:76
  120.8 3.9 %collective-permute-done.1 = bf16[512,3,128]{0,2,1:T(8,128)(2,1)} collective-permute-done((bf16[512,3,128]{0,2,1:T(8,128)(2,1)}, bf16[512,3,128]{0,2,1:T(8,128)(2,1)}, u32[]{:S(2)}, u32[]{:S(2)}) %collective-permute-start.1) | collective-permute-done | bytes 393248 | tf_op jit(solution)/shard_map/ppermute | solution.py:14
  124.8 5.8 %fusion.15 = f32[3,128,512]{2,1,0:T(8,128)S(1)} fusion(f32[3,512,1536]{2,1,0:T(8,128)} %get-tuple-element.7, f32[3,512]{1,0:T(4,128)S(1)} %get-tuple-element.6, bf16[512,3,128]{0,2,1:T(8,128)(2,1)} %get-tuple-element.4, bf16[512,3,128]{0,2,1:T(8,128)(2,1)} %collective-permute-done.1, bf16[512,3,128]{0,2,1:T(8,128)(2,1)} %collective-permute-done), kind=kOutput, calls=%fused_computation.22 | convolution fusion | flops 612630528 | bytes 11409408 | tf_op jit(solution)/shard_map/hij,jhd->ihd/dot_general | solution.py:78
  130.9 1.2 add_convert_fusion
  133.9 20.8 %all-to-all-start = ((bf16[4,64,384]{2,1,0:T(8,128)(2,1)}), bf16[4,64,384]{2,1,0:T(8,128)(2,1)S(1)}, u32[]{:S(2)}, u32[]{:S(2)}) async-start(bf16[4,64,384]{2,1,0:T(8,128)(2,1)} %bitcast.8), calls=%async_computation | async-start | bytes 393216 | tf_op jit(solution)/shard_map/all_to_all | solution.py:100
  154.8 3.0 %copy.37 = bf16[384,3072]{0,1:T(8,128)(2,1)S(1)} copy(bf16[384,3072]{1,0:T(8,128)(2,1)} %param.10) | data formatting | bytes 4718592 | tf_op args[3]
  157.8 2.6 %copy.38 = bf16[384,4,768]{2,0,1:T(8,128)(2,1)} copy(bf16[384,4,768]{0,2,1:T(8,128)(2,1)S(1)} %bitcast.27) | data formatting | bytes 4718592 | tf_op jit(solution)/shard_map/all_to_all | solution.py:20
  160.4 1.7 all-to-all-done
  162.1 3.6 %all-to-all-start.1 = ((bf16[384,4,768]{2,0,1:T(8,128)(2,1)}), bf16[384,4,768]{2,0,1:T(8,128)(2,1)S(1)}, u32[]{:S(2)}, u32[]{:S(2)}) async-start(bf16[384,4,768]{2,0,1:T(8,128)(2,1)} %copy.38), calls=%async_computation.1 | async-start | bytes 4718592 | tf_op jit(solution)/shard_map/all_to_all | solution.py:20
  165.7 35.5 %all_gather.7 = bf16[256,1536]{1,0:T(8,128)(2,1)S(1)} all-gather(bf16[256,384]{1,0:T(8,128)(2,1)S(1)} %bitcast.35), channel_id=1, replica_groups=mesh['seq'=4,'phase'=4,'dp'=2] {'phase'}, dimensions={1}, use_global_device_ids=true | all-gather | bytes 983040 | tf_op jit(solution)/shard_map/all_gather | solution.py:19
  201.2 1.2 copy.36
  202.4 2.2 %convert_reduce_fusion = f32[256,768]{1,0:T(8,128)S(1)} fusion(bf16[256,4,384]{0,2,1:T(8,128)(2,1)} %bitcast.33, bf16[384,4,768]{2,0,1:T(8,128)(2,1)S(1)} %all-to-all-done.1), kind=kOutput, calls=%fused_computation.10 | convolution fusion | flops 606142464 | bytes 3932160 | tf_op jit(solution)/shard_map/nsg,sgc->snc/dot_general | solution.py:24
  204.7 8.2 %psum.7 = f32[256]{0:T(256)S(1)} all-reduce(f32[256]{0:T(256)S(1)} %multiply_reduce_fusion.1), channel_id=1, replica_groups=mesh['seq'=4,'phase'=4,'dp'=2] {'phase'}, use_global_device_ids=true, to_apply=%region_6.7 | all-reduce | flops 256 | bytes 2048 | tf_op jit(solution)/shard_map/psum | solution.py:31
  (37 shorter events, 6.2 us)
Async XLA Ops:
  7.2 2.5 %copy-start = (bf16[512,1536]{1,0:T(8,128)(2,1)S(1)}, bf16[512,1536]{1,0:T(8,128)(2,1)}, u32[]{:S(2)}) copy-start(bf16[512,1536]{1,0:T(8,128)(2,1)} %param.7) | copy-start | bytes 4718596
  7.2 75.0 %all-gather.2.cloned.1.call-start = ((), (), s32[]{:S(2)}) async-start(), calls=%async_computation.2 | async-start | bytes 4423680 | tf_op jit(solution)/shard_map/all_gather | solution.py:47
  9.6 2.1 copy-start.4
  9.6 2.1 copy-start.6
  9.7 72.5 %copy-start.5 = (f32[1536]{0:T(1024)S(1)}, f32[1536]{0:T(1024)}, u32[]{:S(2)}) copy-start(f32[1536]{0:T(1024)} %param.8) | copy-start | bytes 18436
  87.1 13.5 %copy-start.1 = (bf16[512,1152]{0,1:T(8,128)(2,1)}, bf16[512,1152]{0,1:T(8,128)(2,1)S(1)}, u32[]{:S(2)}) copy-start(bf16[512,1152]{0,1:T(8,128)(2,1)S(1)} %copy.32) | copy-start | bytes 3538948
  88.2 12.4 %collective-permute-start.2 = (bf16[512,3,128]{2,0,1:T(8,128)(2,1)S(1)}, bf16[512,3,128]{2,0,1:T(8,128)(2,1)S(1)}, u32[]{:S(2)}, u32[]{:S(2)}) collective-permute-start(bf16[512,3,128]{2,0,1:T(8,128)(2,1)S(1)} %bitcast.30), channel_id=1, source_target_pairs={{0,16},{8,24},{1,17},{9,25},{2,18},{10,26},{3,19},{11,27},{4,20},{... | collective-permute-start | bytes 1179656 | tf_op jit(solution)/shard_map/ppermute | solution.py:14
  91.1 17.9 %collective-permute-start.3 = (bf16[512,3,128]{2,0,1:T(8,128)(2,1)S(1)}, bf16[512,3,128]{2,0,1:T(8,128)(2,1)S(1)}, u32[]{:S(2)}, u32[]{:S(2)}) collective-permute-start(bf16[512,3,128]{2,0,1:T(8,128)(2,1)S(1)} %bitcast.31), channel_id=1, source_target_pairs={{0,8},{8,16},{16,24},{1,9},{9,17},{17,25},{2,10},{10,18},{18,26},{... | collective-permute-start | bytes 1179656 | tf_op jit(solution)/shard_map/ppermute | solution.py:14
  95.3 25.6 %collective-permute-start = (bf16[512,3,128]{0,2,1:T(8,128)(2,1)}, bf16[512,3,128]{0,2,1:T(8,128)(2,1)}, u32[]{:S(2)}, u32[]{:S(2)}) collective-permute-start(bf16[512,3,128]{0,2,1:T(8,128)(2,1)} %get-tuple-element.4), channel_id=1, source_target_pairs={{0,16},{8,24},{1,17},{9,25},{2,18},{10,26},{3,19},{11,27},{4,20},{... | collective-permute-start | bytes 1179656 | tf_op jit(solution)/shard_map/ppermute | solution.py:14
  97.3 27.5 %collective-permute-start.1 = (bf16[512,3,128]{0,2,1:T(8,128)(2,1)}, bf16[512,3,128]{0,2,1:T(8,128)(2,1)}, u32[]{:S(2)}, u32[]{:S(2)}) collective-permute-start(bf16[512,3,128]{0,2,1:T(8,128)(2,1)} %get-tuple-element.4), channel_id=1, source_target_pairs={{0,8},{8,16},{16,24},{1,9},{9,17},{17,25},{2,10},{10,18},{18,26},{... | collective-permute-start | bytes 1179656 | tf_op jit(solution)/shard_map/ppermute | solution.py:14
  132.1 25.7 %copy-start.2 = (bf16[512,384]{1,0:T(8,128)(2,1)}, bf16[512,384]{1,0:T(8,128)(2,1)S(1)}, u32[]{:S(2)}) copy-start(bf16[512,384]{1,0:T(8,128)(2,1)S(1)} %add_convert_fusion) | copy-start | bytes 1179652
  133.9 28.1 %all-to-all-start = ((bf16[4,64,384]{2,1,0:T(8,128)(2,1)}), bf16[4,64,384]{2,1,0:T(8,128)(2,1)S(1)}, u32[]{:S(2)}, u32[]{:S(2)}) async-start(bf16[4,64,384]{2,1,0:T(8,128)(2,1)} %bitcast.8), calls=%async_computation | async-start | bytes 393216 | tf_op jit(solution)/shard_map/all_to_all | solution.py:100
  162.1 40.3 %all-to-all-start.1 = ((bf16[384,4,768]{2,0,1:T(8,128)(2,1)}), bf16[384,4,768]{2,0,1:T(8,128)(2,1)S(1)}, u32[]{:S(2)}, u32[]{:S(2)}) async-start(bf16[384,4,768]{2,0,1:T(8,128)(2,1)} %copy.38), calls=%async_computation.1 | async-start | bytes 4718592 | tf_op jit(solution)/shard_map/all_to_all | solution.py:20
  202.4 10.6 %copy-start.3 = (f32[768]{0:T(1024)S(1)}, f32[768]{0:T(1024)}, u32[]{:S(2)}) copy-start(f32[768]{0:T(1024)} %param.11) | copy-start | bytes 9220
Sparse Core Ops, SparseCore 0:
  9.7 72.4 all-gather.1
where the time goes:
time: 221 us
  waiting for transfers between devices  84.5 us (38%)
  blocking collectives  43.7 us (20%)
  starting transfers between devices  34.5 us (16%)
  other arithmetic  16 us (7%)
  matrix products  15.7 us (7%)
  between operations  14.3 us (6%)
  local copies, waits for them, and re-layouts  12 us (5%)
    all_gather x1, waiting for transfers between devices, on_device(): piece = lax.all_gather(w_qkv, 'seq', axis=0, tiled=True)  69.8 us
    all_gather x1, blocking collectives, project_rows(): full_rows = lax.all_gather(rows, 'phase', axis=1, tiled=True)  35.5 us
    all_to_all x1, starting transfers between devices, on_device(): lax.all_to_all(outgoing, 'seq', split_axis=0, concat_axis=0, tiled=True)  20.8 us
    ppermute x4, waiting for transfers between devices, passed_along(): return lax.ppermute(value, axis, pairs)  13 us
    ppermute x4, starting transfers between devices, passed_along(): return lax.ppermute(value, axis, pairs)  10 us
    sub x1, other arithmetic, on_device(): expo = jnp.exp(scores - top)  9.4 us
    psum x1, blocking collectives, project_rows(): squares = lax.psum(jnp.sum(projected * projected, axis=1), 'phase')  8.21 us
    dot_general x1, matrix products, on_device(): jnp.einsum('hij,jhd->ihd', probs, value_all, preferred_element_type=jnp.f...  5.83 us
  transfers between devices with their start and end apart: 7, of which 5 were waited for; matrix products, arithmetic and copies ran while one was open for 10% of the time, Pallas kernels for 0%

commit v1 on v0

--- a/solution.py
+++ b/solution.py
@@ -1,11 +1,375 @@
+import functools
+import math
 import jax
 import jax.numpy as jnp
 from jax import lax
+from jax.experimental import pallas as pl
+from jax.experimental.pallas import tpu as pltpu
 from jax.sharding import PartitionSpec as P
 
 DC = 3072
 HD = 128
 WINDOW = 1024
+MESH = pl.DeviceIdType.MESH
+NEG = -0.7 * 3.4e38
+
+
+def fused_kernel(
+    dims,
+    x_ref,
+    gain_ref,
+    w_ref,
+    up_ref,
+    og_ref,
+    bounds_ref,
+    ocol_ref,
+    orow_ref,
+    bs_ref,
+    ss_ref,
+    wbuf,
+    upbuf,
+    normed,
+    acc,
+    qbuf,
+    kbuf,
+    vbuf,
+    obuf,
+    mbuf,
+    lbuf,
+    rowbuf,
+    sqbuf,
+    outbuf,
+    loc_sem,
+    w_send,
+    w_recv,
+    p_send,
+    p_recv,
+    up_send,
+    up_recv,
+    kv_send,
+    kv_recv,
+    row_send,
+    row_recv,
+    sq_send,
+    sq_recv,
+    a_send,
+    a_recv,
+):
+    n_seq, n_phase, reach, slot = dims
+    tok, d = x_ref.shape
+    rows = w_ref.shape[0]
+    half = rows // 2
+    width = w_ref.shape[1] // 3
+    heads = width // HD
+    crows = bounds_ref.shape[0]
+    cols = og_ref.shape[1]
+    z = lax.axis_index("seq")
+    p = lax.axis_index("phase")
+    c = lax.axis_index("dp")
+
+    peers = (
+        [{"seq": lax.rem(z + k, n_seq)} for k in range(1, n_seq)]
+        + [{"phase": lax.rem(p + k, n_phase)} for k in range(1, n_phase)]
+        + [{"dp": 1 - c}]
+    )
+    barrier = pltpu.get_barrier_semaphore()
+    for peer in peers:
+        pl.semaphore_signal(barrier, inc=1, device_id=peer, device_id_type=MESH)
+    pl.semaphore_wait(barrier, len(peers))
+
+    pending = []
+
+    def send(src, dst, ssem, rsem, peer, cond=None):
+        copy = pltpu.make_async_remote_copy(
+            src_ref=src, dst_ref=dst, send_sem=ssem, recv_sem=rsem, device_id=peer, device_id_type=MESH
+        )
+        if cond is None:
+            copy.start()
+        else:
+            pl.when(cond)(copy.start)
+        pending.append((cond, copy))
+        return copy
+
+    mine_half = pl.ds(pl.multiple_of(c * half, half), half)
+    right, left = {"seq": z + 1}, {"seq": z - 1}
+    ways = ((right, z < n_seq - 1, -1), (left, z > 0, 1))
+    for way, (peer, cond, sign) in enumerate(ways):
+        send(
+            w_ref.at[mine_half],
+            wbuf.at[z, mine_half],
+            w_send.at[way, 0],
+            w_recv.at[way, 0],
+            peer,
+            cond,
+        )
+    own_w = pltpu.make_async_copy(w_ref, wbuf.at[z], loc_sem.at[0])
+    own_w.start()
+    up_copies = []
+    for k in range(1, n_phase):
+        other = lax.rem(p + k, n_phase)
+        part = pl.ds(pl.multiple_of(other * cols, 128), cols)
+        up_copies.append(
+            send(up_ref.at[:, part], upbuf.at[p], up_send.at[k - 1], up_recv.at[k - 1], {"phase": other})
+        )
+    own_up = pltpu.make_async_copy(
+        up_ref.at[:, pl.ds(pl.multiple_of(p * cols, 128), cols)], upbuf.at[p], loc_sem.at[1]
+    )
+    own_up.start()
+
+    step_rows = 64
+
+    @pl.loop(0, tok // step_rows)
+    def _(i):
+        r = pl.ds(pl.multiple_of(i * step_rows, step_rows), step_rows)
+        xx = x_ref[r, :].astype(jnp.float32)
+        scale = lax.rsqrt(jnp.mean(xx * xx, axis=1, keepdims=True) + 1e-05)
+        normed[r, :] = (xx * scale * gain_ref[...]).astype(jnp.bfloat16)
+
+    def accumulate(shard, first):
+        k = pl.ds(pl.multiple_of(shard * rows, 128), rows)
+
+        @pl.loop(0, 3)
+        def _(j):
+            n = pl.ds(pl.multiple_of(j * width, 128), width)
+            part = jnp.dot(normed[:, k], wbuf[shard, :, n], preferred_element_type=jnp.float32)
+            if first:
+                acc[:, n] = part
+            else:
+                acc[:, n] = acc[:, n] + part
+
+    own_w.wait()
+    accumulate(z, True)
+
+    for t in range(1, n_seq):
+        arrivals = []
+        for way, (peer, cond, sign) in enumerate(ways):
+            shard = z + sign * t
+            there = (shard >= 0) & (shard < n_seq)
+            piece = wbuf.at[jnp.clip(shard, 0, n_seq - 1), mine_half]
+            got = pltpu.make_async_remote_copy(
+                src_ref=piece,
+                dst_ref=piece,
+                send_sem=w_send.at[way, t - 1],
+                recv_sem=w_recv.at[way, t - 1],
+                device_id=peer,
+                device_id_type=MESH,
+            )
+            pl.when(there)(got.wait_recv)
+            if t < n_seq - 1:
+                send(piece, piece, w_send.at[way, t], w_recv.at[way, t], peer, there & cond)
+            twin = send(piece, piece, p_send.at[way, t - 1], p_recv.at[way, t - 1], {"dp": 1 - c}, there)
+            arrivals.append((there, shard, twin))
+        for there, shard, twin in arrivals:
+
+            @pl.when(there)
+            def _():
+                twin.wait_recv()
+                accumulate(shard, False)
+
+    for h in range(heads):
+        kbuf[0, h] = acc[:, width + h * HD : width + (h + 1) * HD].astype(jnp.bfloat16)
+    for h in range(heads):
+        vbuf[0, h] = acc[:, 2 * width + h * HD : 2 * width + (h + 1) * HD].astype(jnp.bfloat16)
+    has_right = z < n_seq - 1
+    kv_copies = {}
+
+    def send_kv(dist, cond):
+        for which, buf in enumerate((kbuf, vbuf)):
+            kv_copies[dist, which] = send(
+                buf.at[dist], buf.at[dist + 1], kv_send.at[which, dist], kv_recv.at[which, dist], right, cond
+            )
+
+    send_kv(0, has_right)
+    for h in range(heads):
+        qbuf[h] = acc[:, h * HD : (h + 1) * HD].astype(jnp.bfloat16)
+
+    tq = min(tok, 256)
+    scale = HD ** (-0.5) * math.log2(math.e)
+
+    def attend(dist):
+        @pl.loop(0, heads * (tok // tq))
+        def _(it):
+            h = it // (tok // tq)
+            q0 = pl.multiple_of((it % (tok // tq)) * tq, tq)
+            r = pl.ds(q0, tq)
+            s = lax.dot_general(
+                qbuf[h, r, :],
+                kbuf[dist, h],
+                (((1,), (1,)), ((), ())),
+                preferred_element_type=jnp.float32,
+            )
+            if dist == 0 or (dist + 1) * tok - 1 >= WINDOW:
+                qi = q0 + lax.broadcasted_iota(jnp.int32, s.shape, 0)
+                kj = lax.broadcasted_iota(jnp.int32, s.shape, 1) - dist * tok
+                s = jnp.where((kj <= qi) & (kj > qi - WINDOW), s, NEG)
+            top = jnp.max(s, axis=1, keepdims=True)
+            if dist > 0:
+                old = mbuf[h, r, :]
+                top = jnp.maximum(top, old)
+            e = jnp.exp2(s * scale - top * scale)
+            total = jnp.sum(e, axis=1, keepdims=True)
+            o = jnp.dot(e.astype(jnp.bfloat16), vbuf[dist, h], preferred_element_type=jnp.float32)
+            if dist > 0:
+                fade = jnp.exp2((old - top) * scale)
+                total = total + fade * lbuf[h, r, :]
+                o = o + fade * obuf[h, r, :]
+            mbuf[h, r, :] = top
+            lbuf[h, r, :] = total
+            obuf[h, r, :] = o
+
+    attend(0)
+    for dist in range(1, reach + 1):
+        there = z >= dist
+
+        @pl.when(there)
+        def _():
+            for which in range(2):
+                kv_copies[dist - 1, which].wait_recv()
+
+        if dist < reach:
+            send_kv(dist, there & has_right)
+
+        @pl.when(there)
+        def _():
+            attend(dist)
+
+    for h in range(heads):
+        res = x_ref[:, pl.ds(pl.multiple_of(p * width + h * HD, HD), HD)].astype(jnp.float32)
+        att = (obuf[h] / lbuf[h]).astype(jnp.bfloat16).astype(jnp.float32)
+        bs_ref[:, h * HD : (h + 1) * HD] = (res + att).astype(jnp.bfloat16)
+
+    local = bounds_ref[...] - z * tok
+    pick = (local == lax.broadcasted_iota(jnp.int32, (crows, tok), 1)).astype(jnp.float32).astype(jnp.bfloat16)
+    rowbuf[p] = jnp.dot(pick, bs_ref[...], preferred_element_type=jnp.float32).astype(jnp.bfloat16)
+    row_copies = []
+    for k in range(1, n_phase):
+        other = lax.rem(p + k, n_phase)
+        row_copies.append(
+            send(rowbuf.at[p], rowbuf.at[p], row_send.at[k - 1], row_recv.at[k - 1], {"phase": other})
+        )
+
+    same = ocol_ref[...] == orow_ref[...]
+    before = lax.broadcasted_iota(jnp.int32, (crows, crows), 0) < lax.broadcasted_iota(
+        jnp.int32, (crows, crows), 1
+    )
+    rank = jnp.sum(jnp.where(same & before, 1, 0), axis=0, keepdims=True)
+    target = orow_ref[...] * slot + rank
+    place = (target == lax.broadcasted_iota(jnp.int32, (n_seq * slot, crows), 0)).astype(jnp.float32).astype(
+        jnp.bfloat16
+    )
+
+    own_up.wait()
+    for copy in up_copies:
+        copy.wait_recv()
+
+    def piece(s):
+        got = jnp.dot(rowbuf[s], upbuf[s], preferred_element_type=jnp.float32)
+        return got.astype(jnp.bfloat16).astype(jnp.float32)
+
+    projected = piece(p)
+    for copy in row_copies:
+        copy.wait_recv()
+    for k in range(1, n_phase):
+        projected = projected + piece(lax.rem(p + k, n_phase))
+    sq = jnp.sum(projected * projected, axis=1, keepdims=True)
+    sqbuf[p] = jnp.broadcast_to(sq, (crows, crows)).T[0:8, :]
+    sq_copies = []
+    for k in range(1, n_phase):
+        other = lax.rem(p + k, n_phase)
+        sq_copies.append(
+            send(sqbuf.at[p], sqbuf.at[p], sq_send.at[k - 1], sq_recv.at[k - 1], {"phase": other})
+        )
+    for copy in sq_copies:
+        copy.wait_recv()
+    all_sq = sqbuf[0]
+    for k in range(1, n_phase):
+        all_sq = all_sq + sqbuf[k]
+    all_sq = jnp.broadcast_to(all_sq[0:1, :], (crows, crows)).T[:, 0:1]
+    norm = lax.rsqrt(all_sq / (n_phase * cols) + 1e-05)
+    main_in = (projected * norm * og_ref[...]).astype(jnp.bfloat16)
+    routed = jnp.dot(place, main_in, preferred_element_type=jnp.float32).astype(jnp.bfloat16)
+    for s in range(n_seq):
+        outbuf[s] = routed[s * slot : (s + 1) * slot]
+    a_copies = []
+    for k in range(1, n_seq):
+        other = lax.rem(z + k, n_seq)
+        a_copies.append(
+            send(outbuf.at[other], ss_ref.at[z], a_send.at[k - 1], a_recv.at[k - 1], {"seq": other})
+        )
+    ss_ref[z] = outbuf[z]
+    for copy in a_copies:
+        copy.wait_recv()
+    for cond, copy in pending:
+        if cond is None:
+            copy.wait_send()
+        else:
+            pl.when(cond)(copy.wait_send)
+
+
+def fused(n_seq, n_phase, byte_embed, in_gain, w_qkv, w_up, out_gain, bounds, owner):
+    tok, d = byte_embed.shape
+    rows, _, width = w_qkv.shape
+    heads = width // HD
+    crows = bounds.shape[0]
+    cols = out_gain.shape[0]
+    slot = 2 * crows // n_seq
+    reach = -(-WINDOW // tok)
+    bf, f32 = jnp.bfloat16, jnp.float32
+    vmem = pl.BlockSpec(memory_space=pltpu.VMEM)
+    hbm = pl.BlockSpec(memory_space=pl.ANY)
+    dma = pltpu.SemaphoreType.DMA
+    states, stretch = pl.pallas_call(
+        functools.partial(fused_kernel, (n_seq, n_phase, reach, slot)),
+        out_shape=(
+            jax.ShapeDtypeStruct((tok, width), bf),
+            jax.ShapeDtypeStruct((n_seq, slot, cols), bf),
+        ),
+        in_specs=[vmem, vmem, hbm, hbm, vmem, vmem, vmem, vmem],
+        out_specs=(vmem, vmem),
+        scratch_shapes=[
+            pltpu.VMEM((n_seq, rows, 3 * width), bf),
+            pltpu.VMEM((n_phase, rows, cols), bf),
+            pltpu.VMEM((tok, d), bf),
+            pltpu.VMEM((tok, 3 * width), f32),
+            pltpu.VMEM((heads, tok, HD), bf),
+            pltpu.VMEM((reach + 1, heads, tok, HD), bf),
+            pltpu.VMEM((reach + 1, heads, tok, HD), bf),
+            pltpu.VMEM((heads, tok, HD), f32),
+            pltpu.VMEM((heads, tok, 1), f32),
+            pltpu.VMEM((heads, tok, 1), f32),
+            pltpu.VMEM((n_phase, crows, width), bf),
+            pltpu.VMEM((n_phase, 8, crows), f32),
+            pltpu.VMEM((n_seq, slot, cols), bf),
+            dma((2,)),
+            dma((2, n_seq - 1)),
+            dma((2, n_seq - 1)),
+            dma((2, n_seq - 1)),
+            dma((2, n_seq - 1)),
+            dma((n_phase - 1,)),
+            dma((n_phase - 1,)),
+            dma((2, reach)),
+            dma((2, reach)),
+            dma((n_phase - 1,)),
+            dma((n_phase - 1,)),
+            dma((n_phase - 1,)),
+            dma((n_phase - 1,)),
+            dma((n_seq - 1,)),
+            dma((n_seq - 1,)),
+        ],
+        compiler_params=pltpu.CompilerParams(
+            collective_id=0, has_side_effects=True, vmem_limit_bytes=48 * 1024 * 1024
+        ),
+    )(
+        byte_embed,
+        in_gain.reshape(1, d),
+        w_qkv.reshape(rows, 3 * width),
+        w_up,
+        out_gain.reshape(1, cols),
+        bounds.reshape(crows, 1),
+        owner,
+        owner.reshape(1, crows),
+    )
+    return states, stretch.reshape(n_seq * slot, cols)
 
 
 def passed_along(value, axis, by):
@@ -105,8 +469,18 @@
 
 
 def solution(mesh):
+    n_seq, n_phase, n_dp = (mesh.shape[axis] for axis in ("seq", "phase", "dp"))
+
+    def body(byte_embed, in_gain, w_qkv, *rest):
+        tok, (rows, _, width) = byte_embed.shape[0], w_qkv.shape
+        slot = 2 * rest[2].shape[0] // n_seq
+        tiled = rows % 128 == 0 and width % HD == 0 and tok % 256 == 0 and slot % 16 == 0
+        if tiled and n_dp == 2 and w_qkv.shape[0] == rest[0].shape[0]:
+            return fused(n_seq, n_phase, byte_embed, in_gain, w_qkv, *rest)
+        return on_device(byte_embed, in_gain, w_qkv, *rest)
+
     return jax.shard_map(
-        on_device,
+        body,
         mesh=mesh,
         in_specs=(
             P(("dp", "seq"), None),

time: 221 us -> 107 us (0.48)
  Pallas kernels: 0 us -> 99.2 us
  waiting for transfers between devices: 84.5 us -> 0 us
  blocking collectives: 43.7 us -> 0 us
  starting transfers between devices: 34.5 us -> 0 us
  other arithmetic: 16 us -> 0 us
  matrix products: 15.7 us -> 0 us
  between operations: 14.3 us -> 0.74 us
  local copies, waits for them, and re-layouts: 12 us -> 7.17 us
    pallas_call x0 -> x1, Pallas kernels: none -> 99.2 us  [fused(): pl.pallas_call(functools.partial(fused_kernel, (n_seq, n_phase, reach, sl...]
    all_gather x1 -> x0, waiting for transfers between devices: 69.8 us -> none  [on_device(): piece = lax.all_gather(w_qkv, 'seq', axis=0, tiled=True)]
    all_gather x1 -> x0, blocking collectives: 35.5 us -> none  [project_rows(): full_rows = lax.all_gather(rows, 'phase', axis=1, tiled=True)]
    all_to_all x2 -> x0, starting transfers between devices: 24.5 us -> none  [the longest x1 20.8 us: on_device(): lax.all_to_all(outgoing, 'seq', split_axis=0, concat_axis=0, tiled=True)]
    dot_general x5 -> x0, matrix products: 15.7 us -> none  [the longest x1 5.83 us: on_device(): jnp.einsum('hij,jhd->ihd', probs, value_all, preferred_element_type=jnp.f...]
    ppermute x4 -> x0, waiting for transfers between devices: 13 us -> none  [passed_along(): return lax.ppermute(value, axis, pairs)]
    ppermute x4 -> x0, starting transfers between devices: 10 us -> none  [passed_along(): return lax.ppermute(value, axis, pairs)]
    sub x1 -> x0, other arithmetic: 9.4 us -> none  [on_device(): expo = jnp.exp(scores - top)]
  transfers between devices with their start and end apart: 7 -> 0, of which waited for: 5 -> 0; matrix products, arithmetic and copies ran while one was open for 10% -> 0% of each run, Pallas kernels for 0% -> 0%
where the time goes in v1:
time: 107 us
  Pallas kernels  99.2 us (93%)
  local copies, waits for them, and re-layouts  7.17 us (7%)
    pallas_call x1, Pallas kernels, fused(): pl.pallas_call(functools.partial(fused_kernel, (n_seq, n_phase, reach, sl...  99.2 us
    unnamed x16, local copies, waits for them, and re-layouts  5.46 us

profile of v1, /device:TPU:0, one launch (start us, length us, event | category | flops | bytes accessed | tf_op | source)
XLA Modules:
  0.0 107.1 jit_solution(3877383423342870620)
XLA Ops:
  0.6 0.0 copy-start.5
  0.6 0.0 copy-start.2
  0.7 0.0 copy-start.3
  0.7 0.0 copy-start.4
  0.7 0.0 copy-start
  0.7 2.4 %copy.12 = bf16[384,3,384]{0,2,1:T(8,128)(2,1)} copy(bf16[384,3,384]{2,0,1:T(8,128)(2,1)} %param.9) | data formatting | bytes 1769472 | tf_op args[2]
  3.1 1.6 %copy.13.w_ref = bf16[384,1152]{1,0:T(8,128)(2,1)S(1)} copy(bf16[384,1152]{0,1:T(8,128)(2,1)} %bitcast.6) | data formatting | bytes 1769472 | tf_op jit(solution)/shard_map/reshape | solution.py:365
  4.7 0.0 copy-done.5
  4.7 0.1 copy.14.bounds_ref
  4.8 0.0 copy-done.2
  4.8 0.1 copy.15.ocol_ref
  4.9 0.0 copy-done.3
  5.0 0.0 copy-done.4
  5.0 0.0 copy-done
  5.0 0.0 copy-start.1
  5.0 1.4 %copy-done.1 = bf16[512,1536]{1,0:T(8,128)(2,1)S(1)} copy-done((bf16[512,1536]{1,0:T(8,128)(2,1)S(1)}, bf16[512,1536]{1,0:T(8,128)(2,1)}, u32[]{:S(2)}) %copy-start.1) | copy-done | bytes 1572888
  6.4 99.2 %shard_map.86 = (bf16[512,384]{1,0:T(8,128)(2,1)S(1)}, bf16[4,64,768]{2,1,0:T(8,128)(2,1)S(1)}) custom-call(bf16[512,1536]{1,0:T(8,128)(2,1)S(1)} %copy-done.1, f32[1,1536]{1,0:T(1,128)S(1)} %reshape.22.gain_ref, bf16[384,1152]{1,0:T(8,128)(2,1)S(1)} %copy.13.w_ref, bf16[384,3072]{1,0:T(8,128)(2,1)S(1)} %copy-done, f32[1,768]{1,0:T(1,128)S(1)} %reshape.24.og_ref, ...), custom_call_target="tpu_custom_call" | custom-call | tf_op jit(solution)/shard_map/pallas_call | solution.py:321
  105.6 0.7 copy.18
  106.4 0.7 copy.19
  (2 shorter events, 0.0 us)
Async XLA Ops:
  0.6 4.1 %copy-start.5 = (s32[128]{0:T(128)S(1)}, s32[128]{0:T(128)}, u32[]{:S(2)}) copy-start(s32[128]{0:T(128)} %param.12) | copy-start | bytes 1540
  0.6 4.2 %copy-start.2 = (s32[128,1]{0,1:T(1,128)S(1)}, s32[128,1]{0,1:T(1,128)}, u32[]{:S(2)}) copy-start(s32[128,1]{0,1:T(1,128)} %param.13) | copy-start | bytes 1540
  0.7 4.3 %copy-start.3 = (f32[1536]{0:T(1024)S(1)}, f32[1536]{0:T(1024)}, u32[]{:S(2)}) copy-start(f32[1536]{0:T(1024)} %param.8) | copy-start | bytes 18436
  0.7 4.3 %copy-start.4 = (f32[768]{0:T(1024)S(1)}, f32[768]{0:T(1024)}, u32[]{:S(2)}) copy-start(f32[768]{0:T(1024)} %param.11) | copy-start | bytes 9220
  0.7 4.3 %copy-start = (bf16[384,3072]{1,0:T(8,128)(2,1)S(1)}, bf16[384,3072]{1,0:T(8,128)(2,1)}, u32[]{:S(2)}) copy-start(bf16[384,3072]{1,0:T(8,128)(2,1)} %up_ref.1) | copy-start | bytes 7077892
  5.0 1.4 %copy-start.1 = (bf16[512,1536]{1,0:T(8,128)(2,1)S(1)}, bf16[512,1536]{1,0:T(8,128)(2,1)}, u32[]{:S(2)}) copy-start(bf16[512,1536]{1,0:T(8,128)(2,1)} %x_ref.1) | copy-start | bytes 4718596

commit v2 on v1

v2 whole, which is shorter than its diff:
```python
import functools
import math
import jax
import jax.numpy as jnp
from jax import lax
from jax.experimental import pallas as pl
from jax.experimental.pallas import tpu as pltpu
from jax.sharding import PartitionSpec as P

DC = 3072
HD = 128
WINDOW = 1024
MESH = pl.DeviceIdType.MESH
NEG = -0.7 * 3.4e38


def fused_kernel(
    dims,
    x_ref,
    gain_ref,
    w_ref,
    up_ref,
    og_ref,
    bounds_ref,
    owner_ref,
    bs_ref,
    ss_ref,
    xbuf,
    normed,
    halo,
    nhalo,
    wbuf,
    upbuf,
    kbuf,
    vbuf,
    obuf,
    mbuf,
    lbuf,
    rowbuf,
    sqbuf,
    outbuf,
    loc_sem,
    w_send,
    w_recv,
    p_send,
    p_recv,
    up_send,
    up_recv,
    upp_send,
    upp_recv,
    h_send,
    h_recv,
    g_send,
    g_recv,
    row_send,
    row_recv,
    sq_send,
    sq_recv,
    a_send,
    a_recv,
):
    n_seq, n_phase, reach, slot = dims
    tok, d = xbuf.shape
    rows, width = w_ref.shape[1:]
    half = rows // 2
    heads = width // HD
    crows = bounds_ref.shape[1]
    cols = og_ref.shape[1]
    z = lax.axis_index("seq")
    p = lax.axis_index("phase")
    c = lax.axis_index("dp")

    own_x = pltpu.make_async_copy(x_ref, xbuf, loc_sem.at[0])
    own_x.start()
    own_up = pltpu.make_async_copy(
        up_ref.at[:, pl.ds(pl.multiple_of(p * cols, 128), cols)], upbuf.at[p], loc_sem.at[1]
    )
    own_up.start()
    own_w = []
    for h in range(heads):
        own_w.append(
            pltpu.make_async_copy(
                w_ref.at[:, :, pl.ds(h * HD, HD)],
                wbuf.at[h, :, pl.ds(pl.multiple_of(z * rows, rows), rows), :],
                loc_sem.at[2 + h],
            )
        )
        own_w[h].start()

    twin_core = {"dp": 1 - c}
    peers = (
        [{"seq": lax.rem(z + k, n_seq)} for k in range(1, n_seq)]
        + [{"phase": lax.rem(p + k, n_phase)} for k in range(1, n_phase)]
        + [twin_core]
    )
    barrier = pltpu.get_barrier_semaphore()
    for peer in peers:
        pl.semaphore_signal(barrier, inc=1, device_id=peer, device_id_type=MESH)
    pl.semaphore_wait(barrier, len(peers))

    pending = []

    def when(cond, action):
        if cond is None:
            action()
        else:
            pl.when(cond)(action)

    def send(src, dst, ssem, rsem, peer, cond=None):
        copy = pltpu.make_async_remote_copy(
            src_ref=src, dst_ref=dst, send_sem=ssem, recv_sem=rsem, device_id=peer, device_id_type=MESH
        )
        when(cond, copy.start)
        pending.append((cond, copy))
        return copy

    right, left = {"seq": z + 1}, {"seq": z - 1}
    has_right, has_left = z < n_seq - 1, z > 0
    ways = ((right, has_right, -1), (left, has_left, 1))

    def chunk(h, shard):
        at = pl.multiple_of(shard * rows + c * half, half)
        return wbuf.at[h, :, pl.ds(at, half), :]

    def issue_own(h):
        src = w_ref.at[:, pl.ds(pl.multiple_of(c * half, half), half), pl.ds(h * HD, HD)]
        for way, (peer, cond, sign) in enumerate(ways):
            send(src, chunk(h, z), w_send.at[way, h, 0], w_recv.at[way, h, 0], peer, cond)

    twins = {}

    def relay(h, t):
        for way, (peer, cond, sign) in enumerate(ways):
            shard = z + sign * t
            there = (shard >= 0) & (shard < n_seq)
            piece = chunk(h, jnp.clip(shard, 0, n_seq - 1))
            got = pltpu.make_async_remote_copy(
                src_ref=piece,
                dst_ref=piece,
                send_sem=w_send.at[way, h, t - 1],
                recv_sem=w_recv.at[way, h, t - 1],
                device_id=peer,
                device_id_type=MESH,
            )
            pl.when(there)(got.wait_recv)
            if t < n_seq - 1:
                send(piece, piece, w_send.at[way, h, t], w_recv.at[way, h, t], peer, there & cond)
            twins[h, t, way] = (
                there,
                send(piece, piece, p_send.at[way, h, t - 1], p_recv.at[way, h, t - 1], twin_core, there),
            )

    def finish(h):
        own_w[h].wait()
        for t in range(1, n_seq):
            for way in range(2):
                there, twin = twins[h, t, way]
                pl.when(there)(twin.wait_recv)

    across = {1: {"phase": p + 1 - 2 * lax.rem(p, 2)}, 2: {"phase": lax.rem(p + 2, n_phase)}}
    spots = {k: v["phase"] for k, v in across.items()}
    mine = {}

    def halo_start(dist, cond):
        src = x_ref.at[:, pl.ds(pl.multiple_of(p * width, 128), width)] if dist == 1 else halo.at[dist - 2, p]
        mine[dist] = send(src, halo.at[dist - 1, p], h_send.at[dist - 1], h_recv.at[dist - 1], right, cond)

    gathers = {}

    def halo_spread(dist):
        there = z >= dist
        pl.when(there)(mine[dist].wait_recv)
        if dist < reach:
            halo_start(dist + 1, there & has_right)
        for k in (1, 2):
            piece = halo.at[dist - 1, p]
            gathers[dist, k] = send(
                piece, piece, g_send.at[dist - 1, k - 1], g_recv.at[dist - 1, k - 1], across[k], there
            )

    def halo_pass(dist):
        there = z >= dist
        for k in (1, 2):
            pl.when(there)(gathers[dist, k].wait_recv)
            part = pl.ds((k - 1) * (tok // 2), tok // 2)
            piece = halo.at[dist - 1, spots[k], part]
            gathers[dist, 2 + k] = send(
                piece, piece, g_send.at[dist - 1, k + 1], g_recv.at[dist - 1, k + 1], across[3 - k], there
            )

    step_rows = 64

    def halo_norm(dist):
        @pl.when(z >= dist)
        def _():
            for k in (1, 2):
                gathers[dist, 2 + k].wait_recv()

            @pl.loop(0, tok // step_rows)
            def _(i):
                r = pl.ds(pl.multiple_of(i * step_rows, step_rows), step_rows)
                xx = jnp.concatenate([halo[dist - 1, s, r, :] for s in range(n_phase)], axis=1).astype(
                    jnp.float32
                )
                scale = lax.rsqrt(jnp.mean(xx * xx, axis=1, keepdims=True) + 1e-05)
                nhalo[dist - 1, r, :] = (xx * scale * gain_ref[...]).astype(jnp.bfloat16)

    halo_start(1, has_right)
    issue_own(0)
    up_rows = up_ref.shape[0] // 2
    up_half = pl.ds(pl.multiple_of(c * up_rows, up_rows), up_rows)
    up_copies, up_twins = [], []
    for k in range(1, n_phase):
        other = lax.rem(p + k, n_phase)
        part = pl.ds(pl.multiple_of(other * cols, 128), cols)
        up_copies.append(
            send(
                up_ref.at[up_half, part],
                upbuf.at[p, up_half],
                up_send.at[k - 1],
                up_recv.at[k - 1],
                {"phase": other},
            )
        )

    own_x.wait()

    @pl.loop(0, tok // step_rows)
    def _(i):
        r = pl.ds(pl.multiple_of(i * step_rows, step_rows), step_rows)
        xx = xbuf[r, :].astype(jnp.float32)
        scale = lax.rsqrt(jnp.mean(xx * xx, axis=1, keepdims=True) + 1e-05)
        normed[r, :] = (xx * scale * gain_ref[...]).astype(jnp.bfloat16)

    def column(ref):
        wide = jnp.broadcast_to(ref[...].astype(jnp.float32), (crows, crows))
        return wide.T

    local = column(bounds_ref)[:, 0:1] - (z * tok).astype(jnp.float32)
    spot = lax.broadcasted_iota(jnp.int32, (crows, tok), 1).astype(jnp.float32)
    pick = jnp.where(local == spot, 1.0, 0.0).astype(jnp.bfloat16)
    same = column(owner_ref) == owner_ref[...].astype(jnp.float32)
    before = lax.broadcasted_iota(jnp.int32, (crows, crows), 0) < lax.broadcasted_iota(
        jnp.int32, (crows, crows), 1
    )
    rank = jnp.sum(jnp.where(same & before, 1, 0), axis=0, keepdims=True)
    target = owner_ref[...] * slot + rank
    place = jnp.where(
        target == lax.broadcasted_iota(jnp.int32, (n_seq * slot, crows), 0), 1.0, 0.0
    ).astype(jnp.bfloat16)

    tq = min(tok, 256)
    scale = HD ** (-0.5) * math.log2(math.e)

    def attend(dist, query):
        for q0 in range(0, tok, tq):
            r = pl.ds(q0, tq)
            keys = tok if dist else q0 + tq
            s = lax.dot_general(
                query[q0 : q0 + tq],
                kbuf[dist, :keys],
                (((1,), (1,)), ((), ())),
                preferred_element_type=jnp.float32,
            )
            if dist == 0 or (dist + 1) * tok - 1 >= WINDOW:
                qi = q0 + lax.broadcasted_iota(jnp.int32, s.shape, 0)
                kj = lax.broadcasted_iota(jnp.int32, s.shape, 1) - dist * tok
                s = jnp.where((kj <= qi) & (kj > qi - WINDOW), s, NEG)
            top = jnp.max(s, axis=1, keepdims=True)
            if dist > 0:
                old = mbuf[r, :]
                top = jnp.maximum(top, old)
            e = jnp.exp2(s * scale - top * scale)
            total = jnp.sum(e, axis=1, keepdims=True)
            o = jnp.dot(e.astype(jnp.bfloat16), vbuf[dist, :keys], preferred_element_type=jnp.float32)
            if dist > 0:
                fade = jnp.exp2((old - top) * scale)
                total = total + fade * lbuf[r, :]
                o = o + fade * obuf[r, :]
            mbuf[r, :] = top
            lbuf[r, :] = total
            obuf[r, :] = o

    def own_block(h):
        w = jnp.concatenate([wbuf[h, j] for j in range(3)], axis=1)
        got = jnp.dot(normed[...], w, preferred_element_type=jnp.float32).astype(jnp.bfloat16)
        qbuf = got[:, :HD]
        kbuf[0] = got[:, HD : 2 * HD]
        vbuf[0] = got[:, 2 * HD :]
        attend(0, qbuf)
        return qbuf

    def earlier_block(h, dist, query):
        @pl.when(z >= dist)
        def _():
            w = jnp.concatenate([wbuf[h, j] for j in range(1, 3)], axis=1)
            got = jnp.dot(nhalo[dist - 1], w, preferred_element_type=jnp.float32).astype(jnp.bfloat16)
            kbuf[dist] = got[:, :HD]
            vbuf[dist] = got[:, HD:]
            attend(dist, query)

    row_copies = []

    def close(h):
        at = slice(h * HD, (h + 1) * HD)
        res = xbuf[:, pl.ds(pl.multiple_of(p * width + h * HD, HD), HD)].astype(jnp.float32)
        att = (obuf[...] / lbuf[...]).astype(jnp.bfloat16).astype(jnp.float32)
        states = (res + att).astype(jnp.bfloat16)
        bs_ref[:, at] = states
        rowbuf[h, p] = jnp.dot(pick, states, preferred_element_type=jnp.float32).astype(jnp.bfloat16)
        for k in range(1, n_phase):
            row_copies.append(
                send(
                    rowbuf.at[h, p],
                    rowbuf.at[h, p],
                    row_send.at[h, k - 1],
                    row_recv.at[h, k - 1],
                    {"phase": lax.rem(p + k, n_phase)},
                )
            )

    halo_spread(1)
    relay(0, 1)
    for dist in range(2, reach + 1):
        halo_spread(dist)
        halo_pass(dist - 1)
    for t in range(2, n_seq):
        relay(0, t)
    if heads > 1:
        issue_own(1)
    halo_pass(reach)
    for k in range(1, n_phase):
        up_copies[k - 1].wait_recv()
        piece = upbuf.at[lax.rem(p + n_phase - k, n_phase), up_half]
        up_twins.append(send(piece, piece, upp_send.at[k - 1], upp_recv.at[k - 1], twin_core))

    for h in range(heads):
        more = list(range(1, n_seq)) if h + 1 < heads else []
        finish(h)
        query = own_block(h)
        for dist in range(1, reach + 1):
            if more:
                relay(h + 1, more.pop(0))
            if h == 0:
                halo_norm(dist)
            earlier_block(h, dist, query)
        for t in more:
            relay(h + 1, t)
        if h + 2 < heads:
            issue_own(h + 2)
        close(h)

    own_up.wait()
    for twin in up_twins:
        twin.wait_recv()

    def piece(s):
        got = jnp.dot(
            jnp.concatenate([rowbuf[h, s] for h in range(heads)], axis=1),
            upbuf[s],
            preferred_element_type=jnp.float32,
        )
        return got.astype(jnp.bfloat16).astype(jnp.float32)

    projected = piece(p)
    for copy in row_copies:
        copy.wait_recv()
    for k in range(1, n_phase):
        projected = projected + piece(lax.rem(p + k, n_phase))
    sq = jnp.sum(projected * projected, axis=1, keepdims=True)
    sqbuf[p] = jnp.broadcast_to(sq, (crows, crows)).T[0:8, :]
    sq_copies = []
    for k in range(1, n_phase):
        other = lax.rem(p + k, n_phase)
        sq_copies.append(
            send(sqbuf.at[p], sqbuf.at[p], sq_send.at[k - 1], sq_recv.at[k - 1], {"phase": other})
        )
    for copy in sq_copies:
        copy.wait_recv()
    all_sq = sqbuf[0]
    for k in range(1, n_phase):
        all_sq = all_sq + sqbuf[k]
    all_sq = jnp.broadcast_to(all_sq[0:1, :], (crows, crows)).T[:, 0:1]
    norm = lax.rsqrt(all_sq / (n_phase * cols) + 1e-05)
    main_in = (projected * norm * og_ref[...]).astype(jnp.bfloat16)
    routed = jnp.dot(place, main_in, preferred_element_type=jnp.float32).astype(jnp.bfloat16)
    for s in range(n_seq):
        outbuf[s] = routed[s * slot : (s + 1) * slot]
    a_copies = []
    for k in range(1, n_seq):
        other = lax.rem(z + k, n_seq)
        a_copies.append(
            send(outbuf.at[other], ss_ref.at[z], a_send.at[k - 1], a_recv.at[k - 1], {"seq": other})
        )
    ss_ref[z] = outbuf[z]
    for copy in a_copies:
        copy.wait_recv()
    for cond, copy in pending:
        when(cond, copy.wait_send)


def fused(n_seq, n_phase, byte_embed, in_gain, w_qkv, w_up, out_gain, bounds, owner):
    tok, d = byte_embed.shape
    rows, _, width = w_qkv.shape
    heads = width // HD
    crows = bounds.shape[0]
    cols = out_gain.shape[0]
    slot = 2 * crows // n_seq
    reach = -(-WINDOW // tok)
    bf, f32 = jnp.bfloat16, jnp.float32
    vmem = pl.BlockSpec(memory_space=pltpu.VMEM)
    hbm = pl.BlockSpec(memory_space=pltpu.HBM)
    dma = pltpu.SemaphoreType.DMA
    states, stretch = pl.pallas_call(
        functools.partial(fused_kernel, (n_seq, n_phase, reach, slot)),
        out_shape=(
            jax.ShapeDtypeStruct((tok, width), bf),
            jax.ShapeDtypeStruct((n_seq, slot, cols), bf),
        ),
        in_specs=[hbm, vmem, hbm, hbm, vmem, vmem, vmem],
        out_specs=(vmem, vmem),
        scratch_shapes=[
            pltpu.VMEM((tok, d), bf),
            pltpu.VMEM((tok, d), bf),
            pltpu.VMEM((reach, n_phase, tok, width), bf),
            pltpu.VMEM((reach, tok, d), bf),
            pltpu.VMEM((heads, 3, n_seq * rows, HD), bf),
            pltpu.VMEM((n_phase, w_up.shape[0], cols), bf),
            pltpu.VMEM((reach + 1, tok, HD), bf),
            pltpu.VMEM((reach + 1, tok, HD), bf),
            pltpu.VMEM((tok, HD), f32),
            pltpu.VMEM((tok, 1), f32),
            pltpu.VMEM((tok, 1), f32),
            pltpu.VMEM((heads, n_phase, crows, HD), bf),
            pltpu.VMEM((n_phase, 8, crows), f32),
            pltpu.VMEM((n_seq, slot, cols), bf),
            dma((2 + heads,)),
            dma((2, heads, n_seq - 1)),
            dma((2, heads, n_seq - 1)),
            dma((2, heads, n_seq - 1)),
            dma((2, heads, n_seq - 1)),
            dma((n_phase - 1,)),
            dma((n_phase - 1,)),
            dma((n_phase - 1,)),
            dma((n_phase - 1,)),
            dma((reach,)),
            dma((reach,)),
            dma((reach, 4)),
            dma((reach, 4)),
            dma((heads, n_phase - 1)),
            dma((heads, n_phase - 1)),
            dma((n_phase - 1,)),
            dma((n_phase - 1,)),
            dma((n_seq - 1,)),
            dma((n_seq - 1,)),
        ],
        compiler_params=pltpu.CompilerParams(
            collective_id=0, has_side_effects=True, vmem_limit_bytes=56 * 1024 * 1024
        ),
    )(
        byte_embed,
        in_gain.reshape(1, d),
        jnp.transpose(w_qkv, (1, 0, 2)),
        w_up,
        out_gain.reshape(1, cols),
        bounds.reshape(1, crows),
        owner.reshape(1, crows),
    )
    return states, stretch.reshape(n_seq * slot, cols)


def passed_along(value, axis, by):
    devices = lax.axis_size(axis)
    pairs = [(i, i + by) for i in range(devices) if 0 <= i + by < devices]
    return lax.ppermute(value, axis, pairs)


def project_rows(rows, w_up, out_gain):
    groups = lax.axis_size("phase")
    full_rows = lax.all_gather(rows, "phase", axis=1, tiled=True)
    w_cols = lax.all_to_all(w_up, "phase", split_axis=1, concat_axis=0, tiled=True)
    count = full_rows.shape[0]
    width = rows.shape[1]
    columns = w_cols.shape[1]
    pieces = jnp.einsum(
        "nsg,sgc->snc",
        full_rows.reshape(count, groups, width),
        w_cols.reshape(groups, width, columns),
        preferred_element_type=jnp.float32,
    )
    projected = jnp.sum(pieces.astype(jnp.bfloat16).astype(jnp.float32), axis=0)
    squares = lax.psum(jnp.sum(projected * projected, axis=1), "phase")
    scale = lax.rsqrt(squares / DC + 1e-05)
    return (projected * scale[:, None] * out_gain).astype(jnp.bfloat16)


def on_device(byte_embed, in_gain, w_qkv, w_up, out_gain, bounds, owner):
    tok = byte_embed.shape[0]
    n_seq = lax.axis_size("seq")
    mine = lax.axis_index("seq")
    section = lax.axis_index("phase")
    width_dev = w_qkv.shape[2]
    heads_dev = width_dev // HD
    x32 = byte_embed.astype(jnp.float32)
    normed = (x32 * lax.rsqrt(jnp.mean(x32 * x32, axis=1, keepdims=True) + 1e-05) * in_gain).astype(
        jnp.bfloat16
    )
    piece = lax.all_gather(w_qkv, "seq", axis=0, tiled=True)
    qkv = jnp.dot(
        normed, piece.reshape(piece.shape[0], 3 * width_dev), preferred_element_type=jnp.float32
    ).astype(jnp.bfloat16)
    qkv = qkv.reshape(tok, 3, heads_dev, HD)
    query = qkv[:, 0]
    keys = qkv[:, 1]
    values = qkv[:, 2]
    reach = -(-WINDOW // tok)
    key_list = [keys]
    value_list = [values]
    for distance in range(1, reach + 1):
        earlier_keys, earlier_values = passed_along((keys, values), "seq", distance)
        key_list = [earlier_keys] + key_list
        value_list = [earlier_values] + value_list
    key_all = jnp.concatenate(key_list, axis=0)
    value_all = jnp.concatenate(value_list, axis=0)
    scores = jnp.einsum(
        "ihd,jhd->hij", query, key_all, preferred_element_type=jnp.float32
    ) * HD ** (-0.5)
    q_pos = mine * tok + jnp.arange(tok, dtype=jnp.int32)
    k_pos = mine * tok - reach * tok + jnp.arange((reach + 1) * tok, dtype=jnp.int32)
    keep = (
        (k_pos[None, :] <= q_pos[:, None])
        & (k_pos[None, :] > q_pos[:, None] - WINDOW)
        & (k_pos[None, :] >= 0)
    )
    scores = jnp.where(keep[None], scores, -jnp.inf)
    top = jnp.max(scores, axis=2, keepdims=True)
    expo = jnp.exp(scores - top)
    probs = (expo / jnp.sum(expo, axis=2, keepdims=True)).astype(jnp.bfloat16)
    attended = jnp.einsum(
        "hij,jhd->ihd", probs, value_all, preferred_element_type=jnp.float32
    ).astype(jnp.bfloat16)
    attended = attended.reshape(tok, width_dev)
    residual = lax.dynamic_slice_in_dim(x32, section * width_dev, width_dev, 1)
    byte_states = (residual + attended.astype(jnp.float32)).astype(jnp.bfloat16)
    local = bounds - mine * tok
    stretch_rows = jnp.take(byte_states, local, axis=0)
    owners = owner[:, 0]
    crows = owners.shape[0]
    slot_count = 2 * crows // n_seq
    place = jnp.arange(crows, dtype=jnp.int32)
    earlier = (owners[:, None] == owners[None, :]) & (place[None, :] < place[:, None])
    rank = jnp.sum(earlier.astype(jnp.int32), axis=1)
    target = owners * slot_count + rank
    placing = (target[None, :] == jnp.arange(n_seq * slot_count, dtype=jnp.int32)[:, None]).astype(
        jnp.bfloat16
    )
    outgoing = jnp.dot(placing, stretch_rows, preferred_element_type=jnp.float32).astype(
        jnp.bfloat16
    )
    outgoing = outgoing.reshape(n_seq, slot_count, width_dev)
    arrived = lax.all_to_all(outgoing, "seq", split_axis=0, concat_axis=0, tiled=True).reshape(
        n_seq * slot_count, width_dev
    )
    stretch_states = project_rows(arrived, w_up, out_gain)
    return (byte_states, stretch_states)


def solution(mesh):
    n_seq, n_phase, n_dp = (mesh.shape[axis] for axis in ("seq", "phase", "dp"))

    def body(byte_embed, in_gain, w_qkv, *rest):
        tok, (rows, _, width) = byte_embed.shape[0], w_qkv.shape
        slot = 2 * rest[2].shape[0] // n_seq
        tiled = rows % 128 == 0 and width % HD == 0 and tok % 256 == 0 and slot % 16 == 0
        if tiled and n_dp == 2 and n_phase == 4 and w_qkv.shape[0] == rest[0].shape[0]:
            return fused(n_seq, n_phase, byte_embed, in_gain, w_qkv, *rest)
        return on_device(byte_embed, in_gain, w_qkv, *rest)

    return jax.shard_map(
        body,
        mesh=mesh,
        in_specs=(
            P(("dp", "seq"), None),
            P(),
            P("seq", None, "phase"),
            P("phase", None),
            P("phase"),
            P(("dp", "seq")),
            P(("dp", "seq"), None),
        ),
        out_specs=(P(("dp", "seq"), "phase"), P(("dp", "seq"), "phase")),
        check_vma=False,
    )
```

time: 107 us -> 91.6 us (0.86)
  Pallas kernels: 99.2 us -> 84.6 us
    pallas_call x1, Pallas kernels: 99.2 us -> 84.6 us  [fused(): pl.pallas_call(functools.partial(fused_kernel, (n_seq, n_phase, reach, sl...]
    unnamed x16 -> x2, local copies, waits for them, and re-layouts: 5.46 us -> 3.55 us
    reshape x2 -> x0, local copies, waits for them, and re-layouts: 1.7 us -> none  [the longest x1 1.59 us: fused(): w_qkv.reshape(rows, 3 * width)]
    reshape x1, local copies, waits for them, and re-layouts: 0.01 us -> 1.29 us  [fused(): in_gain.reshape(1, d)]
    reshape x1, local copies, waits for them, and re-layouts: 0.01 us -> 1.27 us  [fused(): out_gain.reshape(1, cols)]
where the time goes in v2:
time: 91.6 us; the launch traced here: 91.3 us
  Pallas kernels  84.6 us (92%)
  local copies, waits for them, and re-layouts  6.11 us (7%)
    pallas_call x1, Pallas kernels, fused(): pl.pallas_call(functools.partial(fused_kernel, (n_seq, n_phase, reach, sl...  84.6 us
    unnamed x2, local copies, waits for them, and re-layouts  3.55 us

profile of v2, /device:TPU:0, one launch (start us, length us, event | category | flops | bytes accessed | tf_op | source)
XLA Modules:
  0.0 91.3 jit_solution(2971689034003610487)
XLA Ops:
  0.6 1.3 %reshape.20.og_ref = f32[1,768]{1,0:T(1,128)} reshape(f32[768]{0:T(1024)} %param.11) | data formatting | bytes 6144 | tf_op jit(solution)/shard_map/reshape | solution.py:465
  1.9 1.3 %reshape.19.gain_ref = f32[1,1536]{1,0:T(1,128)} reshape(f32[1536]{0:T(1024)} %param.8) | data formatting | bytes 12288 | tf_op jit(solution)/shard_map/reshape | solution.py:462
  3.2 84.6 %shard_map.86 = (bf16[512,384]{1,0:T(8,128)(2,1)}, bf16[4,64,768]{2,1,0:T(8,128)(2,1)}) custom-call(bf16[512,1536]{1,0:T(8,128)(2,1)} %x_ref.1, f32[1,1536]{1,0:T(1,128)} %reshape.19.gain_ref, bf16[3,384,384]{2,1,0:T(8,128)(2,1)} %bitcast.4, bf16[384,3072]{1,0:T(8,128)(2,1)} %up_ref.1, f32[1,768]{1,0:T(1,128)} %reshape.20.og_ref, s32[1,128]{1,0:T(1,128)} %bitcast.6, ...), custom_call_target="tpu_custom_call" | custom-call | tf_op jit(solution)/shard_map/pallas_call | solution.py:414
  87.8 1.8 %copy.11 = bf16[512,384]{1,0:T(8,128)(2,1)} copy(bf16[512,384]{1,0:T(8,128)(2,1)} %get-tuple-element.8) | data formatting | bytes 786432
  89.5 1.8 %copy.12 = bf16[256,768]{1,0:T(8,128)(2,1)} copy(bf16[256,768]{1,0:T(8,128)(2,1)} %bitcast.5) | data formatting | bytes 786432

commit v3 on v2

--- a/solution.py
+++ b/solution.py
@@ -123,14 +123,22 @@
         return wbuf.at[h, :, pl.ds(at, half), :]
 
     def issue_own(h):
+        if h >= heads or h in issued:
+            return
+        issued.add(h)
         src = w_ref.at[:, pl.ds(pl.multiple_of(c * half, half), half), pl.ds(h * HD, HD)]
         for way, (peer, cond, sign) in enumerate(ways):
             send(src, chunk(h, z), w_send.at[way, h, 0], w_recv.at[way, h, 0], peer, cond)
 
     twins = {}
-
-    def relay(h, t):
-        for way, (peer, cond, sign) in enumerate(ways):
+    issued = set()
+    LEFTWARD, RIGHTWARD = 1, 0
+
+    def relay(h, t, *which):
+        for way in which:
+            if h >= heads or t >= n_seq or (h, t, way) in twins:
+                continue
+            peer, cond, sign = ways[way]
             shard = z + sign * t
             there = (shard >= 0) & (shard < n_seq)
             piece = chunk(h, jnp.clip(shard, 0, n_seq - 1))
@@ -152,6 +160,8 @@
 
     def finish(h):
         own_w[h].wait()
+        for t in range(1, n_seq):
+            relay(h, t, LEFTWARD, RIGHTWARD)
         for t in range(1, n_seq):
             for way in range(2):
                 there, twin = twins[h, t, way]
@@ -319,35 +329,39 @@
                 )
             )
 
+    relay(0, 1, LEFTWARD)
     halo_spread(1)
-    relay(0, 1)
+    issue_own(1)
+    relay(0, 1, RIGHTWARD)
+    for t in range(2, n_seq):
+        relay(0, t, LEFTWARD)
     for dist in range(2, reach + 1):
         halo_spread(dist)
         halo_pass(dist - 1)
-    for t in range(2, n_seq):
-        relay(0, t)
-    if heads > 1:
-        issue_own(1)
-    halo_pass(reach)
+    relay(1, 1, LEFTWARD, RIGHTWARD)
+    issue_own(2)
+    relay(0, 2, RIGHTWARD)
     for k in range(1, n_phase):
         up_copies[k - 1].wait_recv()
         piece = upbuf.at[lax.rem(p + n_phase - k, n_phase), up_half]
         up_twins.append(send(piece, piece, upp_send.at[k - 1], upp_recv.at[k - 1], twin_core))
+    for t in range(2, n_seq):
+        relay(1, t, LEFTWARD)
 
     for h in range(heads):
-        more = list(range(1, n_seq)) if h + 1 < heads else []
+        issue_own(h + 1)
         finish(h)
         query = own_block(h)
+        relay(h + 2, 1, LEFTWARD, RIGHTWARD)
+        if h == 0:
+            halo_pass(reach)
+        relay(h + 1, 2, LEFTWARD, RIGHTWARD)
         for dist in range(1, reach + 1):
-            if more:
-                relay(h + 1, more.pop(0))
             if h == 0:
                 halo_norm(dist)
             earlier_block(h, dist, query)
-        for t in more:
-            relay(h + 1, t)
-        if h + 2 < heads:
-            issue_own(h + 2)
+        relay(h + 2, 2, LEFTWARD, RIGHTWARD)
+        issue_own(h + 3)
         close(h)
 
     own_up.wait()
@@ -455,13 +469,13 @@
             dma((n_seq - 1,)),
         ],
         compiler_params=pltpu.CompilerParams(
-            collective_id=0, has_side_effects=True, vmem_limit_bytes=56 * 1024 * 1024
+            collective_id=0, has_side_effects=True, vmem_limit_bytes=36 * 1024 * 1024
         ),
     )(
-        byte_embed,
+        pltpu.with_memory_space_constraint(byte_embed, pltpu.HBM),
         in_gain.reshape(1, d),
-        jnp.transpose(w_qkv, (1, 0, 2)),
-        w_up,
+        pltpu.with_memory_space_constraint(jnp.transpose(w_qkv, (1, 0, 2)), pltpu.HBM),
+        pltpu.with_memory_space_constraint(w_up, pltpu.HBM),
         out_gain.reshape(1, cols),
         bounds.reshape(1, crows),
         owner.reshape(1, crows),

time: 91.6 us -> 89.2 us (0.974)
  local copies, waits for them, and re-layouts: 6.11 us -> 4.19 us
    unnamed x2 -> x6, local copies, waits for them, and re-layouts: 3.55 us -> 2.8 us
where the time goes in v3:
time: 89.2 us; the launch traced here: 89 us
  Pallas kernels  84.1 us (94%)
  local copies, waits for them, and re-layouts  4.19 us (5%)
    pallas_call x1, Pallas kernels, fused(): pl.pallas_call(functools.partial(fused_kernel, (n_seq, n_phase, reach, sl...  84.1 us
    unnamed x6, local copies, waits for them, and re-layouts  2.8 us

profile of v3, /device:TPU:0, one launch (start us, length us, event | category | flops | bytes accessed | tf_op | source)
XLA Modules:
  0.0 89.0 jit_solution(374232674338432922)
XLA Ops:
  0.6 0.7 reshape.20.og_ref
  1.3 0.7 reshape.19.gain_ref
  2.0 0.0 copy-start
  2.0 0.7 copy-done
  2.7 0.0 copy-start.1
  2.7 0.7 copy-done.1
  3.3 84.1 %shard_map.86 = (bf16[512,384]{1,0:T(8,128)(2,1)S(1)}, bf16[4,64,768]{2,1,0:T(8,128)(2,1)S(1)}) custom-call(bf16[512,1536]{1,0:T(8,128)(2,1)} %x_ref.1, f32[1,1536]{1,0:T(1,128)S(1)} %reshape.19.gain_ref, bf16[3,384,384]{2,1,0:T(8,128)(2,1)} %bitcast.7, bf16[384,3072]{1,0:T(8,128)(2,1)} %up_ref.1, f32[1,768]{1,0:T(1,128)S(1)} %reshape.20.og_ref, ...), custom_call_target="tpu_custom_call" | custom-call | tf_op jit(solution)/shard_map/pallas_call | solution.py:428
  87.5 0.7 copy.11
  88.2 0.7 copy.12
Async XLA Ops:
  2.0 0.7 copy-start
  2.7 0.7 copy-start.1

commit v4 on v3

--- a/solution.py
+++ b/solution.py
@@ -28,9 +28,9 @@
     xbuf,
     normed,
     halo,
-    nhalo,
     wbuf,
     upbuf,
+    qbuf,
     kbuf,
     vbuf,
     obuf,
@@ -172,7 +172,8 @@
     mine = {}
 
     def halo_start(dist, cond):
-        src = x_ref.at[:, pl.ds(pl.multiple_of(p * width, 128), width)] if dist == 1 else halo.at[dist - 2, p]
+        own = normed.at[:, pl.ds(pl.multiple_of(p * width, 128), width)]
+        src = own if dist == 1 else halo.at[dist - 2, p]
         mine[dist] = send(src, halo.at[dist - 1, p], h_send.at[dist - 1], h_recv.at[dist - 1], right, cond)
 
     gathers = {}
@@ -198,24 +199,12 @@
                 piece, piece, g_send.at[dist - 1, k + 1], g_recv.at[dist - 1, k + 1], across[3 - k], there
             )
 
-    step_rows = 64
-
-    def halo_norm(dist):
+    def halo_wait(dist):
         @pl.when(z >= dist)
         def _():
             for k in (1, 2):
                 gathers[dist, 2 + k].wait_recv()
 
-            @pl.loop(0, tok // step_rows)
-            def _(i):
-                r = pl.ds(pl.multiple_of(i * step_rows, step_rows), step_rows)
-                xx = jnp.concatenate([halo[dist - 1, s, r, :] for s in range(n_phase)], axis=1).astype(
-                    jnp.float32
-                )
-                scale = lax.rsqrt(jnp.mean(xx * xx, axis=1, keepdims=True) + 1e-05)
-                nhalo[dist - 1, r, :] = (xx * scale * gain_ref[...]).astype(jnp.bfloat16)
-
-    halo_start(1, has_right)
     issue_own(0)
     up_rows = up_ref.shape[0] // 2
     up_half = pl.ds(pl.multiple_of(c * up_rows, up_rows), up_rows)
@@ -234,6 +223,7 @@
         )
 
     own_x.wait()
+    step_rows = 64
 
     @pl.loop(0, tok // step_rows)
     def _(i):
@@ -242,6 +232,9 @@
         scale = lax.rsqrt(jnp.mean(xx * xx, axis=1, keepdims=True) + 1e-05)
         normed[r, :] = (xx * scale * gain_ref[...]).astype(jnp.bfloat16)
 
+    relay(0, 1, LEFTWARD)
+    halo_start(1, has_right)
+
     def column(ref):
         wide = jnp.broadcast_to(ref[...].astype(jnp.float32), (crows, crows))
         return wide.T
@@ -262,12 +255,12 @@
     tq = min(tok, 256)
     scale = HD ** (-0.5) * math.log2(math.e)
 
-    def attend(dist, query):
+    def attend(dist, h):
         for q0 in range(0, tok, tq):
             r = pl.ds(q0, tq)
             keys = tok if dist else q0 + tq
             s = lax.dot_general(
-                query[q0 : q0 + tq],
+                qbuf[h, r, :],
                 kbuf[dist, :keys],
                 (((1,), (1,)), ((), ())),
                 preferred_element_type=jnp.float32,
@@ -278,43 +271,43 @@
                 s = jnp.where((kj <= qi) & (kj > qi - WINDOW), s, NEG)
             top = jnp.max(s, axis=1, keepdims=True)
             if dist > 0:
-                old = mbuf[r, :]
+                old = mbuf[h, r, :]
                 top = jnp.maximum(top, old)
             e = jnp.exp2(s * scale - top * scale)
             total = jnp.sum(e, axis=1, keepdims=True)
             o = jnp.dot(e.astype(jnp.bfloat16), vbuf[dist, :keys], preferred_element_type=jnp.float32)
             if dist > 0:
                 fade = jnp.exp2((old - top) * scale)
-                total = total + fade * lbuf[r, :]
-                o = o + fade * obuf[r, :]
-            mbuf[r, :] = top
-            lbuf[r, :] = total
-            obuf[r, :] = o
+                total = total + fade * lbuf[h, r, :]
+                o = o + fade * obuf[h, r, :]
+            mbuf[h, r, :] = top
+            lbuf[h, r, :] = total
+            obuf[h, r, :] = o
 
     def own_block(h):
         w = jnp.concatenate([wbuf[h, j] for j in range(3)], axis=1)
         got = jnp.dot(normed[...], w, preferred_element_type=jnp.float32).astype(jnp.bfloat16)
-        qbuf = got[:, :HD]
+        qbuf[h] = got[:, :HD]
         kbuf[0] = got[:, HD : 2 * HD]
         vbuf[0] = got[:, 2 * HD :]
-        attend(0, qbuf)
-        return qbuf
-
-    def earlier_block(h, dist, query):
+        attend(0, h)
+
+    def earlier_block(h, dist):
         @pl.when(z >= dist)
         def _():
             w = jnp.concatenate([wbuf[h, j] for j in range(1, 3)], axis=1)
-            got = jnp.dot(nhalo[dist - 1], w, preferred_element_type=jnp.float32).astype(jnp.bfloat16)
+            rows_in = jnp.concatenate([halo[dist - 1, q] for q in range(n_phase)], axis=1)
+            got = jnp.dot(rows_in, w, preferred_element_type=jnp.float32).astype(jnp.bfloat16)
             kbuf[dist] = got[:, :HD]
             vbuf[dist] = got[:, HD:]
-            attend(dist, query)
+            attend(dist, h)
 
     row_copies = []
 
     def close(h):
         at = slice(h * HD, (h + 1) * HD)
         res = xbuf[:, pl.ds(pl.multiple_of(p * width + h * HD, HD), HD)].astype(jnp.float32)
-        att = (obuf[...] / lbuf[...]).astype(jnp.bfloat16).astype(jnp.float32)
+        att = (obuf[h] / lbuf[h]).astype(jnp.bfloat16).astype(jnp.float32)
         states = (res + att).astype(jnp.bfloat16)
         bs_ref[:, at] = states
         rowbuf[h, p] = jnp.dot(pick, states, preferred_element_type=jnp.float32).astype(jnp.bfloat16)
@@ -329,7 +322,6 @@
                 )
             )
 
-    relay(0, 1, LEFTWARD)
     halo_spread(1)
     issue_own(1)
     relay(0, 1, RIGHTWARD)
@@ -351,17 +343,20 @@
     for h in range(heads):
         issue_own(h + 1)
         finish(h)
-        query = own_block(h)
+        own_block(h)
         relay(h + 2, 1, LEFTWARD, RIGHTWARD)
         if h == 0:
             halo_pass(reach)
         relay(h + 1, 2, LEFTWARD, RIGHTWARD)
-        for dist in range(1, reach + 1):
+        for dist in range(1, reach):
             if h == 0:
-                halo_norm(dist)
-            earlier_block(h, dist, query)
+                halo_wait(dist)
+            earlier_block(h, dist)
         relay(h + 2, 2, LEFTWARD, RIGHTWARD)
         issue_own(h + 3)
+    halo_wait(reach)
+    for h in range(heads):
+        earlier_block(h, reach)
         close(h)
 
     own_up.wait()
@@ -437,14 +432,14 @@
             pltpu.VMEM((tok, d), bf),
             pltpu.VMEM((tok, d), bf),
             pltpu.VMEM((reach, n_phase, tok, width), bf),
-            pltpu.VMEM((reach, tok, d), bf),
             pltpu.VMEM((heads, 3, n_seq * rows, HD), bf),
             pltpu.VMEM((n_phase, w_up.shape[0], cols), bf),
+            pltpu.VMEM((heads, tok, HD), bf),
             pltpu.VMEM((reach + 1, tok, HD), bf),
             pltpu.VMEM((reach + 1, tok, HD), bf),
-            pltpu.VMEM((tok, HD), f32),
-            pltpu.VMEM((tok, 1), f32),
-            pltpu.VMEM((tok, 1), f32),
+            pltpu.VMEM((heads, tok, HD), f32),
+            pltpu.VMEM((heads, tok, 1), f32),
+            pltpu.VMEM((heads, tok, 1), f32),
             pltpu.VMEM((heads, n_phase, crows, HD), bf),
             pltpu.VMEM((n_phase, 8, crows), f32),
             pltpu.VMEM((n_seq, slot, cols), bf),

time: 89.2 us -> 87.2 us (0.978)
  Pallas kernels: 84.1 us -> 82.1 us
    pallas_call x1, Pallas kernels: 84.1 us -> 82.1 us  [fused(): pl.pallas_call(functools.partial(fused_kernel, (n_seq, n_phase, reach, sl...]
where the time goes in v4:
time: 87.2 us; the launch traced here: 86.9 us
  Pallas kernels  82.1 us (94%)
  local copies, waits for them, and re-layouts  4.19 us (5%)
    pallas_call x1, Pallas kernels, fused(): pl.pallas_call(functools.partial(fused_kernel, (n_seq, n_phase, reach, sl...  82.1 us
    unnamed x6, local copies, waits for them, and re-layouts  2.8 us

profile of v4, /device:TPU:0, one launch (start us, length us, event | category | flops | bytes accessed | tf_op | source)
XLA Modules:
  0.0 86.9 jit_solution(18384395429029177955)
XLA Ops:
  0.6 0.7 reshape.20.og_ref
  1.3 0.7 reshape.19.gain_ref
  2.0 0.0 copy-start
  2.0 0.7 copy-done
  2.7 0.0 copy-start.1
  2.7 0.7 copy-done.1
  3.3 82.1 %shard_map.86 = (bf16[512,384]{1,0:T(8,128)(2,1)S(1)}, bf16[4,64,768]{2,1,0:T(8,128)(2,1)S(1)}) custom-call(bf16[512,1536]{1,0:T(8,128)(2,1)} %x_ref.1, f32[1,1536]{1,0:T(1,128)S(1)} %reshape.19.gain_ref, bf16[3,384,384]{2,1,0:T(8,128)(2,1)} %bitcast.7, bf16[384,3072]{1,0:T(8,128)(2,1)} %up_ref.1, f32[1,768]{1,0:T(1,128)S(1)} %reshape.20.og_ref, ...), custom_call_target="tpu_custom_call" | custom-call | tf_op jit(solution)/shard_map/pallas_call | solution.py:423
  85.4 0.7 copy.11
  86.2 0.7 copy.12
Async XLA Ops:
  2.0 0.7 copy-start
  2.7 0.7 copy-start.1
